TPU v7x, 32 devices: a whole 2x2x4 slice. The times are simulated.
32 devices in a mesh: row: 2 (over y), col: 16 (over z, x, core).
Axes of the slice: x: 2, y: 2, z: 4, core: 2. Of those that a mesh axis runs over, the one named last changes fastest.
Arguments:
- tokens: bfloat16 [512, 1024], P(('row', 'col')), may hold values from -6 to 6
- grad_out: bfloat16 [512, 1024], P(('row', 'col')), may hold values from -1.1953125 to 1.1953125
- gains: float32 [2, 1024], replicated, may hold values from 0.1 to 1.9
- flat_in: bfloat16 [16384, 2048], P(('row', 'col')), may hold values from -0.1875 to 0.1875
- flat_out: bfloat16 [16384, 2048], P(('row', 'col')), may hold values from -0.03125 to 0.03125
- flat_moment: float32 [2, 16384, 2048], P(None, ('row', 'col')), may hold values from -3 to 3
- flat_second: float32 [2, 16384, 2048], P(None, ('row', 'col')), may hold values from 0.05 to 2
- tile_in: bfloat16 [16, 6, 256, 2048], P('col', 'row'), may hold values from -0.1875 to 0.1875
- tile_out: bfloat16 [16, 6, 256, 2048], P('col', 'row'), may hold values from -0.03125 to 0.03125
- tile_moment: float32 [2, 16, 6, 256, 2048], P(None, 'col', 'row'), may hold values from -3 to 3
- tile_second: float32 [2, 16, 6, 256, 2048], P(None, 'col', 'row'), may hold values from 0.05 to 2
- owners: int32 [2, 16, 4], P(None, 'col'), may hold values from 0 to 1, as said below
Outputs:
- hidden_out: bfloat16 [512, 1024], P(('row', 'col'))
- grad_tokens: bfloat16 [512, 1024], P(('row', 'col'))
- new_flat_in: bfloat16 [16384, 2048], P(('row', 'col'))
- new_flat_out: bfloat16 [16384, 2048], P(('row', 'col'))
- new_flat_moment: float32 [2, 16384, 2048], P(None, ('row', 'col'))
- new_flat_second: float32 [2, 16384, 2048], P(None, ('row', 'col'))
- new_tile_in: bfloat16 [16, 6, 256, 2048], P('col', 'row')
- new_tile_out: bfloat16 [16, 6, 256, 2048], P('col', 'row')
- new_tile_moment: float32 [2, 16, 6, 256, 2048], P(None, 'col', 'row')
- new_tile_second: float32 [2, 16, 6, 256, 2048], P(None, 'col', 'row')
Inputs may be any that keep to these rules, and one draw needn't show every extreme that they name: `owners`: for each matrix and column block, entry k names the row that owns tile k; each row owns at most 3 tiles of a block and matrix, and in each block and matrix some row owns exactly 3.
All inputs are finite; a program needn't handle non-finite values.
Results may differ from a plain program's by a relative error of at most 0.029.
Values may be sent and summed in bfloat16 or wider, within the bound.
A program may use at most 192 MiB of HBM per device.

v0:
```python
import jax
import jax.numpy as jnp
from jax import lax
from jax.sharding import PartitionSpec as P

norm_eps = 1e-06
beta_one = 0.9
beta_two = 0.95
learn_rate = 0.002
decay_rate = 0.1
adam_eps = 1e-08
gelu_coef = 0.7978845608


def gelu_value(hidden):
    tanh_term = jnp.tanh(gelu_coef * (hidden + 0.044715 * hidden * hidden * hidden))
    return 0.5 * hidden * (1.0 + tanh_term)


def gelu_slope(hidden):
    tanh_term = jnp.tanh(gelu_coef * (hidden + 0.044715 * hidden * hidden * hidden))
    return 0.5 * (1.0 + tanh_term) + 0.5 * hidden * (1.0 - tanh_term * tanh_term) * gelu_coef * (
        1.0 + 0.134145 * hidden * hidden
    )


def adam_update(weight, gradient, moment, second):
    new_moment = beta_one * moment + (1.0 - beta_one) * gradient
    new_second = beta_two * second + (1.0 - beta_two) * gradient * gradient
    weight_float = weight.astype(jnp.float32)
    stepped = weight_float - learn_rate * (
        new_moment / (jnp.sqrt(new_second) + adam_eps) + decay_rate * weight_float
    )
    return (stepped.astype(jnp.bfloat16), new_moment, new_second)


def slot_tables(owner_rows, slot_cap, row_total):
    tile_count = owner_rows.shape[-1]
    positions = jnp.arange(tile_count, dtype=jnp.int32)
    same_owner = owner_rows[..., :, None] == owner_rows[..., None, :]
    earlier = positions[None, :] < positions[:, None]
    tile_rank = jnp.sum(jnp.where(same_owner & earlier, 1, 0), axis=-1).astype(jnp.int32)
    slot_dest = owner_rows * slot_cap + tile_rank
    slot_ids = jnp.arange(row_total * slot_cap, dtype=jnp.int32)
    matches = slot_dest[..., None, :] == slot_ids[:, None]
    slot_tile = jnp.sum(jnp.where(matches, positions, 0), axis=-1)
    slot_live = jnp.any(matches, axis=-1)
    return (slot_dest, slot_tile, slot_live)


def forward(layer_in, gain_vec, w_in, w_out):
    tok_float = layer_in.astype(jnp.float32)
    inv_rms = lax.rsqrt(jnp.mean(tok_float * tok_float, axis=1, keepdims=True) + norm_eps)
    normed = (tok_float * inv_rms * gain_vec).astype(jnp.bfloat16)
    normed_all = lax.all_gather(normed, "col", axis=0, tiled=True)
    hidden = jnp.dot(normed_all, w_in, preferred_element_type=jnp.float32)
    activated = gelu_value(hidden).astype(jnp.bfloat16)
    mixed_sum = lax.psum_scatter(
        lax.dot_general(
            activated, w_out, (((1,), (1,)), ((), ())), preferred_element_type=jnp.float32
        ).astype(jnp.bfloat16),
        "col",
        scatter_dimension=0,
        tiled=True,
    ).astype(jnp.float32)
    return (
        (tok_float + mixed_sum).astype(jnp.bfloat16),
        (tok_float, inv_rms, normed_all, hidden, activated),
    )


def backward(cotangent, gain_vec, w_in, w_out, saved_state):
    tok_float, inv_rms, normed_all, hidden, activated = saved_state
    grad_all = lax.all_gather(cotangent, "col", axis=0, tiled=True)
    d_act = jnp.dot(grad_all, w_out, preferred_element_type=jnp.float32)
    d_hidden = (d_act * gelu_slope(hidden)).astype(jnp.bfloat16)
    d_normed = lax.psum_scatter(
        lax.dot_general(
            d_hidden, w_in, (((1,), (1,)), ((), ())), preferred_element_type=jnp.float32
        ).astype(jnp.bfloat16),
        "col",
        scatter_dimension=0,
        tiled=True,
    ).astype(jnp.float32)
    gated = d_normed * gain_vec
    tok_grad = (
        cotangent.astype(jnp.float32)
        + inv_rms * gated
        - tok_float
        * inv_rms
        * inv_rms
        * inv_rms
        * jnp.mean(tok_float * gated, axis=1, keepdims=True)
    )
    return (tok_grad.astype(jnp.bfloat16), grad_all, d_hidden)


def group_grads(normed_all, d_hidden, grad_all, activated):
    grad_in = lax.dot_general(
        normed_all, d_hidden, (((0,), (0,)), ((), ())), preferred_element_type=jnp.float32
    )
    grad_wout = lax.dot_general(
        grad_all, activated, (((0,), (0,)), ((), ())), preferred_element_type=jnp.float32
    )
    return (grad_in, grad_wout)


def band_sum(left_groups, right_groups, band_index, tile_rows):
    band_cols = lax.dynamic_slice_in_dim(left_groups, band_index * tile_rows, tile_rows, 2)
    products = jnp.einsum(
        "gtr,gtc->grc", band_cols, right_groups, preferred_element_type=jnp.float32
    )
    rounded = lax.optimization_barrier(products.astype(jnp.bfloat16))
    return jnp.sum(rounded.astype(jnp.float32), axis=0)


def shards(
    tokens,
    grad_out,
    gains,
    flat_in,
    flat_out,
    flat_moment,
    flat_second,
    tile_in,
    tile_out,
    tile_moment,
    tile_second,
    owners,
):
    row_total = lax.axis_size("row")
    col_total = lax.axis_size("col")
    row_index = lax.axis_index("row")
    model_width = tokens.shape[1]
    block_width = flat_in.shape[1]
    part_rows = flat_in.shape[0] // col_total
    slot_cap = tile_in.shape[1]
    tile_rows = tile_in.shape[2]
    owner_rows = owners[:, 0, :]
    slot_dest, slot_tile, slot_live = slot_tables(owner_rows, slot_cap, row_total)
    shaped = (
        flat_in.reshape(part_rows, col_total, block_width),
        flat_out.reshape(part_rows, col_total, block_width),
    )
    arrived = (
        lax.all_to_all(shaped[0], "col", split_axis=1, concat_axis=0, tiled=True),
        lax.all_to_all(shaped[1], "col", split_axis=1, concat_axis=0, tiled=True),
    )
    banded = (
        arrived[0].reshape(col_total * part_rows, block_width),
        arrived[1].reshape(col_total * part_rows, block_width),
    )
    whole_weights = (
        lax.all_gather(banded[0], "row", axis=0, tiled=True),
        lax.all_gather(banded[1], "row", axis=0, tiled=True),
    )
    first_in, first_out = (whole_weights[0], whole_weights[1])
    middle, saved_one = forward(tokens, gains[0], first_in, first_out)
    whole_slots = (
        lax.all_gather(tile_in[0], "row", axis=0, tiled=True),
        lax.all_gather(tile_out[0], "row", axis=0, tiled=True),
    )
    second_in = jnp.take(whole_slots[0], slot_dest[0], axis=0).reshape(model_width, block_width)
    second_out = jnp.take(whole_slots[1], slot_dest[1], axis=0).reshape(model_width, block_width)
    hidden_out, saved_two = forward(middle, gains[1], second_in, second_out)
    grad_mid, grad_all_two, d_hidden_two = backward(
        grad_out, gains[1], second_in, second_out, saved_two
    )
    gathered = (
        lax.all_gather(saved_two[2], "row", axis=0, tiled=True),
        lax.all_gather(d_hidden_two, "row", axis=0, tiled=True),
        lax.all_gather(grad_all_two, "row", axis=0, tiled=True),
        lax.all_gather(saved_two[4], "row", axis=0, tiled=True),
    )
    group_tok = saved_two[2].shape[0]
    normed_groups = gathered[0].reshape(row_total, group_tok, model_width)
    hidden_groups = gathered[1].reshape(row_total, group_tok, block_width)
    grad_groups = gathered[2].reshape(row_total, group_tok, model_width)
    act_groups = gathered[3].reshape(row_total, group_tok, block_width)
    my_tiles = lax.dynamic_slice_in_dim(slot_tile, row_index * slot_cap, slot_cap, 1)
    in_list = []
    out_list = []
    for slot_idx in range(slot_cap):
        in_list.append(band_sum(normed_groups, hidden_groups, my_tiles[0, slot_idx], tile_rows))
        out_list.append(band_sum(grad_groups, act_groups, my_tiles[1, slot_idx], tile_rows))
    tile_grad_in = jnp.stack(in_list)
    tile_grad_out = jnp.stack(out_list)
    grad_tokens, grad_all_one, d_hidden_one = backward(
        grad_mid, gains[0], first_in, first_out, saved_one
    )
    grad_in_one, grad_wout_one = group_grads(saved_one[2], d_hidden_one, grad_all_one, saved_one[4])
    banded_sums = (
        lax.psum_scatter(
            grad_in_one.astype(jnp.bfloat16), "row", scatter_dimension=0, tiled=True
        ).astype(jnp.float32),
        lax.psum_scatter(
            grad_wout_one.astype(jnp.bfloat16), "row", scatter_dimension=0, tiled=True
        ).astype(jnp.float32),
    )
    shaped_sums = (
        banded_sums[0].reshape(col_total, part_rows, 1, block_width),
        banded_sums[1].reshape(col_total, part_rows, 1, block_width),
    )
    owned_rows = (
        lax.all_to_all(
            shaped_sums[0].astype(jnp.bfloat16), "col", split_axis=0, concat_axis=2, tiled=True
        ).astype(jnp.float32),
        lax.all_to_all(
            shaped_sums[1].astype(jnp.bfloat16), "col", split_axis=0, concat_axis=2, tiled=True
        ).astype(jnp.float32),
    )
    flat_grad_in = owned_rows[0].reshape(part_rows * col_total, block_width)
    flat_grad_out = owned_rows[1].reshape(part_rows * col_total, block_width)
    new_flat_in, moment_in, second_in_f = adam_update(
        flat_in, flat_grad_in, flat_moment[0], flat_second[0]
    )
    new_flat_out, moment_out, second_out_f = adam_update(
        flat_out, flat_grad_out, flat_moment[1], flat_second[1]
    )
    live_mine = lax.dynamic_slice_in_dim(slot_live, row_index * slot_cap, slot_cap, 1)
    live_in_mine = live_mine[0][:, None, None]
    live_out_mine = live_mine[1][:, None, None]
    upd_in, tmom_in, tsec_in = adam_update(
        tile_in[0], tile_grad_in, tile_moment[0, 0], tile_second[0, 0]
    )
    upd_out, tmom_out, tsec_out = adam_update(
        tile_out[0], tile_grad_out, tile_moment[1, 0], tile_second[1, 0]
    )
    new_tile_in = jnp.where(live_in_mine, upd_in, tile_in[0])[None]
    new_tile_out = jnp.where(live_out_mine, upd_out, tile_out[0])[None]
    new_tmom = jnp.stack(
        [
            jnp.where(live_in_mine, tmom_in, tile_moment[0, 0]),
            jnp.where(live_out_mine, tmom_out, tile_moment[1, 0]),
        ]
    )[:, None]
    new_tsec = jnp.stack(
        [
            jnp.where(live_in_mine, tsec_in, tile_second[0, 0]),
            jnp.where(live_out_mine, tsec_out, tile_second[1, 0]),
        ]
    )[:, None]
    return (
        hidden_out,
        grad_tokens,
        new_flat_in,
        new_flat_out,
        jnp.stack([moment_in, moment_out]),
        jnp.stack([second_in_f, second_out_f]),
        new_tile_in,
        new_tile_out,
        new_tmom,
        new_tsec,
    )


def solution(mesh):
    return jax.shard_map(
        shards,
        mesh=mesh,
        in_specs=(
            P(("row", "col"), None),
            P(("row", "col"), None),
            P(),
            P(("row", "col"), None),
            P(("row", "col"), None),
            P(None, ("row", "col"), None),
            P(None, ("row", "col"), None),
            P("col", "row", None, None),
            P("col", "row", None, None),
            P(None, "col", "row", None, None),
            P(None, "col", "row", None, None),
            P(None, "col", None),
        ),
        out_specs=(
            P(("row", "col"), None),
            P(("row", "col"), None),
            P(("row", "col"), None),
            P(("row", "col"), None),
            P(None, ("row", "col"), None),
            P(None, ("row", "col"), None),
            P("col", "row", None, None),
            P("col", "row", None, None),
            P(None, "col", "row", None, None),
            P(None, "col", "row", None, None),
        ),
        check_vma=False,
    )
```

profile of v0, /device:TPU:0, one launch (start us, length us, event | category | flops | bytes accessed | tf_op | source)
XLA Modules:
  0.0 900.6 jit_solution(14548941014218153708)
XLA Ops:
  9.9 54.6 %all_to_all.48 = bf16[32,16,2048]{2,0,1:T(8,128)(2,1)} all-to-all(bf16[32,16,2048]{2,0,1:T(8,128)(2,1)S(1)} %copy.87), channel_id=1, replica_groups=mesh['row'=2,'col'=16] {'col'}, dimensions={1} | all-to-all | bytes 4194304 | tf_op jit(solution)/shard_map/all_to_all | solution.py:146
  65.8 52.3 %all_to_all.49 = bf16[32,16,2048]{2,0,1:T(8,128)(2,1)} all-to-all(bf16[32,16,2048]{2,0,1:T(8,128)(2,1)S(1)} %copy.88), channel_id=1, replica_groups=mesh['row'=2,'col'=16] {'col'}, dimensions={1} | all-to-all | bytes 4194304 | tf_op jit(solution)/shard_map/all_to_all | solution.py:147
  118.7 22.3 %all_gather.36 = bf16[256,1024]{1,0:T(8,128)(2,1)S(1)} all-gather(bf16[16,1024]{1,0:T(8,128)(2,1)S(1)} %fusion.60), channel_id=1, replica_groups=mesh['row'=2,'col'=16] {'col'}, dimensions={0}, use_global_device_ids=true | all-gather | bytes 557056 | tf_op jit(solution)/shard_map/all_gather | solution.py:55
  141.0 18.9 %all_gather.42 = bf16[256,1024]{1,0:T(8,128)(2,1)S(1)} all-gather(bf16[16,1024]{1,0:T(8,128)(2,1)S(1)} %copy-done.14), channel_id=1, replica_groups=mesh['row'=2,'col'=16] {'col'}, dimensions={0}, use_global_device_ids=true | all-gather | bytes 557056 | tf_op jit(solution)/shard_map/all_gather | solution.py:74
  159.9 5.8 gather_fusion.1
  165.7 8.9 all-gather.23.cloned.1.call-done
  174.6 5.6 gather_fusion
  180.2 52.7 %all-gather.11.cloned.1.call-done = bf16[1024,2048]{1,0:T(8,128)(2,1)} async-done(((bf16[512,2048]{1,0:T(8,128)(2,1)}), bf16[1024,2048]{1,0:T(8,128)(2,1)}) %all-gather.11.cloned.1.call-update) | async-done | bytes 4194320 | tf_op jit(solution)/shard_map/all_gather | solution.py:154
  237.6 53.4 %all-gather.13.cloned.1.call-done = bf16[1024,2048]{1,0:T(8,128)(2,1)} async-done(((bf16[512,2048]{1,0:T(8,128)(2,1)}), bf16[1024,2048]{1,0:T(8,128)(2,1)}) %all-gather.13.cloned.1.call-update) | async-done | bytes 4194320 | tf_op jit(solution)/shard_map/all_gather | solution.py:155
  296.2 7.7 broadcast_select_fusion
  303.8 48.6 %reduce-scatter.7.cloned.1.call-done = bf16[16,1024]{1,0:T(8,128)(2,1)} async-done(((bf16[256,1024]{1,0:T(8,128)(2,1)}), bf16[16,1024]{1,0:T(8,128)(2,1)}) %reduce-scatter.7.cloned.1.call-update) | async-done | bytes 32784 | tf_op jit(solution)/shard_map/reduce_scatter | solution.py:58
  353.5 21.0 %all_gather.39 = bf16[256,1024]{1,0:T(8,128)(2,1)S(1)} all-gather(bf16[16,1024]{1,0:T(8,128)(2,1)S(1)} %fusion.55), channel_id=1, replica_groups=mesh['row'=2,'col'=16] {'col'}, dimensions={0}, use_global_device_ids=true | all-gather | bytes 557056 | tf_op jit(solution)/shard_map/all_gather | solution.py:55
  389.9 49.1 %reduce-scatter.11.cloned.1.call-done = bf16[16,1024]{1,0:T(8,128)(2,1)} async-done(((bf16[256,1024]{1,0:T(8,128)(2,1)}), bf16[16,1024]{1,0:T(8,128)(2,1)}) %reduce-scatter.11.cloned.1.call-update) | async-done | bytes 32784 | tf_op jit(solution)/shard_map/reduce_scatter | solution.py:77
  440.0 58.5 %reduce-scatter.9.cloned.1.call-done = bf16[16,1024]{1,0:T(8,128)(2,1)} async-done(((bf16[256,1024]{1,0:T(8,128)(2,1)}), bf16[16,1024]{1,0:T(8,128)(2,1)}) %reduce-scatter.9.cloned.1.call-update) | async-done | bytes 32784 | tf_op jit(solution)/shard_map/reduce_scatter | solution.py:58
  499.8 20.8 %all_gather.43 = bf16[256,1024]{1,0:T(8,128)(2,1)S(1)} all-gather(bf16[16,1024]{1,0:T(8,128)(2,1)S(1)} %get-tuple-element.33), channel_id=1, replica_groups=mesh['row'=2,'col'=16] {'col'}, dimensions={0}, use_global_device_ids=true | all-gather | bytes 557056 | tf_op jit(solution)/shard_map/all_gather | solution.py:74
  520.7 5.1 fusion.34
  544.1 37.4 %reduce-scatter.13.cloned.1.call-done = bf16[16,1024]{1,0:T(8,128)(2,1)} async-done(((bf16[256,1024]{1,0:T(8,128)(2,1)}), bf16[16,1024]{1,0:T(8,128)(2,1)}) %reduce-scatter.13.cloned.1.call-update) | async-done | bytes 32784 | tf_op jit(solution)/shard_map/reduce_scatter | solution.py:77
  583.9 20.1 %all-gather.19.cloned.1.call-done = bf16[512,1024]{1,0:T(8,128)(2,1)} async-done(((bf16[256,1024]{1,0:T(8,128)(2,1)}), bf16[512,1024]{1,0:T(8,128)(2,1)}) %all-gather.19.cloned.1.call-update) | async-done | bytes 1048592 | tf_op jit(solution)/shard_map/all_gather | solution.py:172
  604.0 35.1 %all-gather.21.cloned.1.call-done = bf16[512,2048]{1,0:T(8,128)(2,1)} async-done(((bf16[256,2048]{1,0:T(8,128)(2,1)}), bf16[512,2048]{1,0:T(8,128)(2,1)}) %all-gather.21.cloned.1.call-update) | async-done | bytes 2097168 | tf_op jit(solution)/shard_map/all_gather | solution.py:173
  645.8 50.5 %reduce-scatter.17.cloned.1.call-done = bf16[512,2048]{1,0:T(8,128)(2,1)} async-done(((bf16[1024,2048]{1,0:T(8,128)(2,1)}), bf16[512,2048]{1,0:T(8,128)(2,1)}) %reduce-scatter.17.cloned.1.call-update) | async-done | bytes 2097168 | tf_op jit(solution)/shard_map/reduce_scatter | solution.py:196
  696.4 5.7 all-to-all-start.3
  702.0 17.0 %all-gather.15.cloned.1.call-done = bf16[512,1024]{1,0:T(8,128)(2,1)} async-done(((bf16[256,1024]{1,0:T(8,128)(2,1)}), bf16[512,1024]{1,0:T(8,128)(2,1)}) %all-gather.15.cloned.1.call-update) | async-done | bytes 1048592 | tf_op jit(solution)/shard_map/all_gather | solution.py:170
  719.1 35.2 %all-gather.17.cloned.1.call-done = bf16[512,2048]{1,0:T(8,128)(2,1)} async-done(((bf16[256,2048]{1,0:T(8,128)(2,1)}), bf16[512,2048]{1,0:T(8,128)(2,1)}) %all-gather.17.cloned.1.call-update) | async-done | bytes 2097168 | tf_op jit(solution)/shard_map/all_gather | solution.py:171
  771.0 14.7 %bitcast_select_fusion.3 = (f32[1,3,256,2048]{3,2,1,0:T(8,128)}, f32[1,3,256,2048]{3,2,1,0:T(8,128)}, f32[1,3,256,2048]{3,2,1,0:T(8,128)}, f32[1,3,256,2048]{3,2,1,0:T(8,128)}) fusion(f32[2,1,3,256,2048]{4,3,2,1,0:T(8,128)S(1)} %bitcast.179, pred[3]{0:T(512)(128)(4,1)S(1)} %get-tuple-element.46, f32[1,1,256,2048]{3,2,1,0:T(8,128)} %bitcast.194, ...), kind=kLoop, calls=%fused_computation.29 | loop fusion | flops 34603008 | bytes 62914568 | tf_op jit(solution)/shard_map/jit(_where)/select_n | solution.py:233
  785.7 25.8 %reduce-scatter.15.cloned.1.call-done = bf16[512,2048]{1,0:T(8,128)(2,1)} async-done(((bf16[1024,2048]{1,0:T(8,128)(2,1)}), bf16[512,2048]{1,0:T(8,128)(2,1)}) %reduce-scatter.15.cloned.1.call-update) | async-done | bytes 2097168 | tf_op jit(solution)/shard_map/reduce_scatter | solution.py:193
  811.4 5.9 all-to-all-start.2
  817.4 11.7 %maximum_bitcast_fusion = f32[2,1,3,256,2048]{4,3,2,1,0:T(8,128)} fusion(f32[1,3,256,2048]{3,2,1,0:T(8,128)} %get-tuple-element.24, f32[1,3,256,2048]{3,2,1,0:T(8,128)} %get-tuple-element.23), kind=kLoop, calls=%fused_computation.2 | loop fusion | flops 3145728 | bytes 25165824 | tf_op jit(solution)/shard_map/broadcast_in_dim | solution.py:231
  829.1 9.2 %maximum_bitcast_fusion.1 = f32[2,1,3,256,2048]{4,3,2,1,0:T(8,128)} fusion(f32[1,3,256,2048]{3,2,1,0:T(8,128)S(1)} %bitcast.187, f32[1,3,256,2048]{3,2,1,0:T(8,128)} %get-tuple-element.26), kind=kLoop, calls=%fused_computation.3 | loop fusion | flops 3145728 | bytes 25165824 | tf_op jit(solution)/shard_map/broadcast_in_dim | solution.py:237
  838.3 20.4 %fusion.10 = (bf16[1,3,256,2048]{3,2,1,0:T(8,128)(2,1)}, bf16[1,3,256,2048]{3,2,1,0:T(8,128)(2,1)}) fusion(bf16[1,3,256,2048]{3,2,1,0:T(8,128)(2,1)} %param.22, pred[3]{0:T(512)(128)(4,1)S(1)} %get-tuple-element.45, f32[1,1,256,2048]{3,2,1,0:T(8,128)} %bitcast.189, f32[1,1,256,2048]{3,2,1,0:T(8,128)} %bitcast.193, f32[1,1,256,2048]{3,2,1,0:T(8,128)} %bitcast.191, ...), kind=kLoop, calls=%fused_computation.40 | loop fusion | flops 56623104 | bytes 50331656 | tf_op jit(solution)/shard_map/jit(_where)/select_n | solution.py:230
  858.8 11.0 %fusion.29 = (f32[1,512,2048]{2,1,0:T(8,128)S(1)}, f32[1,512,2048]{2,1,0:T(8,128)S(1)}, f32[1,512,2048]{2,1,0:T(8,128)S(1)}, f32[1,512,2048]{2,1,0:T(8,128)}) fusion(f32[2,512,2048]{2,1,0:T(8,128)} %param.19, bf16[16,32,1,2048]{3,1,2,0:T(8,128)(2,1)} %all-to-all-done.2, bf16[16,32,1,2048]{3,1,2,0:T(8,128)(2,1)} %all-to-all-done.3, f32[2,512,2048]{2,1,0:T(8,128)} %param.20), kind=kLoop, calls=%fused_computation.61 | loop fusion | flops 16777216 | bytes 37748736 | tf_op jit(solution)/shard_map/add | solution.py:28
  874.6 7.2 pad_maximum_fusion.1
  881.8 11.8 %fusion.17 = (bf16[512,2048]{1,0:T(8,128)(2,1)}, bf16[512,2048]{1,0:T(8,128)(2,1)}) fusion(bf16[512,2048]{1,0:T(8,128)(2,1)} %param.18, f32[2,512,2048]{2,1,0:T(8,128)S(1)} %bitcast.183, f32[2,512,2048]{2,1,0:T(8,128)S(1)} %bitcast.185, bf16[16,32,1,2048]{3,1,2,0:T(8,128)(2,1)} %all-to-all-done.3, bf16[16,32,1,2048]{3,1,2,0:T(8,128)(2,1)} %all-to-all-done.2, ...), kind=kLoop, calls=%fused_computation.47 | loop fusion | flops 33554432 | bytes 29360128 | tf_op jit(solution)/shard_map/convert_element_type | solution.py:34
  (146 shorter events, 77.9 us)
Async XLA Ops:
  7.2 152.7 %all-gather.25.cloned.1.call-start = ((), (), s32[]{:S(2)}) async-start(), calls=%async_computation.23 | async-start | bytes 9437184 | tf_op jit(solution)/shard_map/all_gather | solution.py:161
  7.9 166.7 %all-gather.23.cloned.1.call-start = ((), (), s32[]{:S(2)}) async-start(), calls=%async_computation.22 | async-start | bytes 9437184 | tf_op jit(solution)/shard_map/all_gather | solution.py:160
  8.7 224.2 %all-gather.11.cloned.1.call-start = ((), (), s32[]{:S(2)}) async-start(), calls=%async_computation.10 | async-start | bytes 6291456 | tf_op jit(solution)/shard_map/all_gather | solution.py:154
  9.9 54.7 %copy-start.3 = (bf16[512,2048]{1,0:T(8,128)(2,1)S(1)}, bf16[512,2048]{1,0:T(8,128)(2,1)}, u32[]{:S(2)}) copy-start(bf16[512,2048]{1,0:T(8,128)(2,1)} %param.18) | copy-start | bytes 6291460
  64.5 226.5 %all-gather.13.cloned.1.call-start = ((), (), s32[]{:S(2)}) async-start(), calls=%async_computation.11 | async-start | bytes 6291456 | tf_op jit(solution)/shard_map/all_gather | solution.py:155
  65.8 52.5 %copy-start.15 = (s32[2,1,4]{2,1,0:T(1,128)S(1)}, s32[2,1,4]{2,1,0:T(1,128)}, u32[]{:S(2)}) copy-start(s32[2,1,4]{2,1,0:T(1,128)} %param.25) | copy-start | bytes 100
  65.8 52.7 %copy-start.11 = (bf16[16,1024]{1,0:T(8,128)(2,1)S(1)}, bf16[16,1024]{1,0:T(8,128)(2,1)}, u32[]{:S(2)}) copy-start(bf16[16,1024]{1,0:T(8,128)(2,1)} %param.14) | copy-start | bytes 98308
  65.8 52.9 %copy-start.16 = (f32[2,1024]{1,0:T(2,128)S(1)}, f32[2,1024]{1,0:T(2,128)}, u32[]{:S(2)}) copy-start(f32[2,1024]{1,0:T(2,128)} %param.16) | copy-start | bytes 24580
  65.8 75.2 %copy-start.14 = (bf16[16,1024]{1,0:T(8,128)(2,1)S(1)}, bf16[16,1024]{1,0:T(8,128)(2,1)}, u32[]{:S(2)}) copy-start(bf16[16,1024]{1,0:T(8,128)(2,1)} %param.15) | copy-start | bytes 98308
  118.2 234.3 %reduce-scatter.7.cloned.1.call-start = ((), (), s32[]{:S(2)}) async-start(), calls=%async_computation.12 | async-start | bytes 557056 | tf_op jit(solution)/shard_map/reduce_scatter | solution.py:58
  159.9 218.7 %copy-start.7 = (bf16[256,1024]{1,0:T(8,128)(2,1)}, bf16[256,1024]{1,0:T(8,128)(2,1)S(1)}, u32[]{:S(2)}) copy-start(bf16[256,1024]{1,0:T(8,128)(2,1)S(1)} %all_gather.42) | copy-start | bytes 1572868
  296.1 142.9 %reduce-scatter.11.cloned.1.call-start = ((), (), s32[]{:S(2)}) async-start(), calls=%async_computation.14 | async-start | bytes 557056 | tf_op jit(solution)/shard_map/reduce_scatter | solution.py:77
  380.8 9.0 %copy-start.9 = (bf16[256,2048]{1,0:T(8,128)(2,1)}, bf16[256,2048]{1,0:T(8,128)(2,1)S(1)}, u32[]{:S(2)}) copy-start(bf16[256,2048]{1,0:T(8,128)(2,1)S(1)} %fusion.33) | copy-start | bytes 3145732
  385.5 112.9 %reduce-scatter.9.cloned.1.call-start = ((), (), s32[]{:S(2)}) async-start(), calls=%async_computation.13 | async-start | bytes 557056 | tf_op jit(solution)/shard_map/reduce_scatter | solution.py:58
  389.9 191.7 %reduce-scatter.13.cloned.1.call-start = ((), (), s32[]{:S(2)}) async-start(), calls=%async_computation.15 | async-start | bytes 557056 | tf_op jit(solution)/shard_map/reduce_scatter | solution.py:77
  527.9 76.0 %all-gather.19.cloned.1.call-start = ((), (), s32[]{:S(2)}) async-start(), calls=%async_computation.20 | async-start | bytes 1572864 | tf_op jit(solution)/shard_map/all_gather | solution.py:172
  528.7 110.4 %all-gather.21.cloned.1.call-start = ((), (), s32[]{:S(2)}) async-start(), calls=%async_computation.21 | async-start | bytes 3145728 | tf_op jit(solution)/shard_map/all_gather | solution.py:173
  529.3 167.1 %reduce-scatter.17.cloned.1.call-start = ((), (), s32[]{:S(2)}) async-start(), calls=%async_computation.17 | async-start | bytes 6291456 | tf_op jit(solution)/shard_map/reduce_scatter | solution.py:196
  534.4 184.7 %all-gather.15.cloned.1.call-start = ((), (), s32[]{:S(2)}) async-start(), calls=%async_computation.18 | async-start | bytes 1572864 | tf_op jit(solution)/shard_map/all_gather | solution.py:170
  534.9 219.4 %all-gather.17.cloned.1.call-start = ((), (), s32[]{:S(2)}) async-start(), calls=%async_computation.19 | async-start | bytes 3145728 | tf_op jit(solution)/shard_map/all_gather | solution.py:171
  535.7 275.8 %reduce-scatter.15.cloned.1.call-start = ((), (), s32[]{:S(2)}) async-start(), calls=%async_computation.16 | async-start | bytes 6291456 | tf_op jit(solution)/shard_map/reduce_scatter | solution.py:193
  604.0 37.7 %copy-start.12 = (bf16[512,1024]{1,0:T(8,128)(2,1)S(1)}, bf16[512,1024]{1,0:T(8,128)(2,1)}, u32[]{:S(2)}) copy-start(bf16[512,1024]{1,0:T(8,128)(2,1)} %all-gather.19.cloned.1.call-done) | copy-start | bytes 3145732
  696.4 115.1 %all-to-all-start.3 = ((bf16[16,32,1,2048]{3,1,2,0:T(8,128)(2,1)}), bf16[16,32,1,2048]{3,1,2,0:T(8,128)(2,1)}, u32[]{:S(2)}, u32[]{:S(2)}) async-start(bf16[16,32,1,2048]{3,1,2,0:T(8,128)(2,1)} %bitcast.218), calls=%async_computation.9 | async-start | bytes 4194304 | tf_op jit(solution)/shard_map/all_to_all | solution.py:208
  719.1 37.8 %copy-start.13 = (bf16[512,1024]{1,0:T(8,128)(2,1)S(1)}, bf16[512,1024]{1,0:T(8,128)(2,1)}, u32[]{:S(2)}) copy-start(bf16[512,1024]{1,0:T(8,128)(2,1)} %all-gather.15.cloned.1.call-done) | copy-start | bytes 3145732
  754.3 14.8 %slice-start.3 = ((s8[12582912]{0:T(1024)(128)(4,1)}), s8[4194304]{0:T(1024)(128)(4,1)S(1)}, s32[]{:S(2)}) async-start(s8[12582912]{0:T(1024)(128)(4,1)} %bitcast.180), calls=%async_computation.27 | async-start | bytes 8388608
  757.7 11.5 %slice-start.4 = ((s8[12582912]{0:T(1024)(128)(4,1)}), s8[4194304]{0:T(1024)(128)(4,1)S(1)}, s32[]{:S(2)}) async-start(s8[12582912]{0:T(1024)(128)(4,1)} %bitcast.180), calls=%async_computation.28 | async-start | bytes 8388608
  758.5 10.7 %slice-start = ((s8[12582912]{0:T(1024)(128)(4,1)}), s8[4194304]{0:T(1024)(128)(4,1)S(1)}, s32[]{:S(2)}) async-start(s8[12582912]{0:T(1024)(128)(4,1)} %bitcast.178), calls=%async_computation.24 | async-start | bytes 8388608
  811.4 47.3 %all-to-all-start.2 = ((bf16[16,32,1,2048]{3,1,2,0:T(8,128)(2,1)}), bf16[16,32,1,2048]{3,1,2,0:T(8,128)(2,1)}, u32[]{:S(2)}, u32[]{:S(2)}) async-start(bf16[16,32,1,2048]{3,1,2,0:T(8,128)(2,1)} %bitcast.219), calls=%async_computation.7 | async-start | bytes 4194304 | tf_op jit(solution)/shard_map/all_to_all | solution.py:205
  817.4 11.7 %slice-start.10 = ((s8[6291456]{0:T(1024)(128)(4,1)}), s8[4194304]{0:T(1024)(128)(4,1)S(1)}, s32[]{:S(2)}) async-start(s8[6291456]{0:T(1024)(128)(4,1)} %bitcast.186), calls=%async_computation.34 | async-start | bytes 8388608
  817.4 11.7 %slice-start.11 = ((s8[6291456]{0:T(1024)(128)(4,1)}), s8[2097152]{0:T(1024)(128)(4,1)S(1)}, s32[]{:S(2)}) async-start(s8[6291456]{0:T(1024)(128)(4,1)} %bitcast.186), calls=%async_computation.35 | async-start | bytes 4194304
  869.8 12.0 %slice-start.6 = ((s8[8388608]{0:T(1024)(128)(4,1)}), s8[4194304]{0:T(1024)(128)(4,1)S(1)}, s32[]{:S(2)}) async-start(s8[8388608]{0:T(1024)(128)(4,1)} %bitcast.182), calls=%async_computation.30 | async-start | bytes 8388608
  869.8 12.0 %slice-start.8 = ((s8[8388608]{0:T(1024)(128)(4,1)}), s8[4194304]{0:T(1024)(128)(4,1)S(1)}, s32[]{:S(2)}) async-start(s8[8388608]{0:T(1024)(128)(4,1)} %bitcast.184), calls=%async_computation.32 | async-start | bytes 8388608
  (14 other events, 67.3 us)
Sparse Core Ops, SparseCore 0:
  9.5 83.0 all-gather.24
  94.2 80.3 all-gather.22
  176.1 56.7 all-gather.10
  234.3 56.7 all-gather.12
  296.3 56.1 reduce-scatter.6
  385.6 53.3 reduce-scatter.10
  443.2 55.1 reduce-scatter.8
  528.1 53.4 reduce-scatter.12
  583.7 20.2 all-gather.18
  605.9 33.0 all-gather.20
  641.9 54.3 reduce-scatter.16
  697.8 21.2 all-gather.14
  721.2 33.0 all-gather.16
  757.0 54.3 reduce-scatter.14
where the time goes:
time: 913 us; the launch traced here: 901 us
  waiting for transfers between devices  496 us (54%)
  blocking collectives  190 us (21%)
  other arithmetic  115 us (13%)
  matrix products  51.5 us (6%)
  between operations  18.7 us (2%)
  local copies, waits for them, and re-layouts  16.5 us (2%)
  starting transfers between devices  12.4 us (1%)
    reduce_scatter x2, waiting for transfers between devices, forward(): lax.psum_scatter(lax.dot_general(activated, w_out, (((1,), (1,)), ((), ()...  107 us
    reduce_scatter x2, waiting for transfers between devices, backward(): lax.psum_scatter(lax.dot_general(d_hidden, w_in, (((1,), (1,)), ((), ()))...  86.5 us
    all_to_all x1, blocking collectives, shards(): lax.all_to_all(shaped[0], 'col', split_axis=1, concat_axis=0, tiled=True)  54.6 us
    all_gather x1, waiting for transfers between devices, shards(): lax.all_gather(banded[1], 'row', axis=0, tiled=True)  53.4 us
    all_gather x1, waiting for transfers between devices, shards(): lax.all_gather(banded[0], 'row', axis=0, tiled=True)  52.7 us
    all_to_all x1, blocking collectives, shards(): lax.all_to_all(shaped[1], 'col', split_axis=1, concat_axis=0, tiled=True)  52.3 us
    reduce_scatter x1, waiting for transfers between devices, shards(): lax.psum_scatter(grad_wout_one.astype(jnp.bfloat16), 'row', scatter_dimen...  50.5 us
    all_gather x2, blocking collectives, forward(): normed_all = lax.all_gather(normed, 'col', axis=0, tiled=True)  43.3 us
  transfers between devices with their start and end apart: 16, of which 13 were waited for; matrix products, arithmetic and copies ran while one was open for 13% of the time, Pallas kernels for 0%

commit v1 on v0

v1 whole, which is shorter than its diff:
```python
import jax
import jax.numpy as jnp
from jax import lax
from jax.experimental import pallas as pl
from jax.experimental.pallas import tpu as pltpu
from jax.sharding import PartitionSpec as P

norm_eps = 1e-06
beta_one = 0.9
beta_two = 0.95
learn_rate = 0.002
decay_rate = 0.1
adam_eps = 1e-08
gelu_coef = 0.7978845608
both = ("row", "col")


def gelu_both(hidden):
    square = hidden * hidden
    tanh_term = jnp.tanh(gelu_coef * (hidden + 0.044715 * square * hidden))
    value = 0.5 * hidden * (1.0 + tanh_term)
    slope = 0.5 * (1.0 + tanh_term) + 0.5 * hidden * (1.0 - tanh_term * tanh_term) * gelu_coef * (
        1.0 + 0.134145 * square
    )
    return value, slope


def adam_update(weight, gradient, moment, second):
    new_moment = beta_one * moment + (1.0 - beta_one) * gradient
    new_second = beta_two * second + (1.0 - beta_two) * gradient * gradient
    weight_float = weight.astype(jnp.float32)
    stepped = weight_float - learn_rate * (
        new_moment / (jnp.sqrt(new_second) + adam_eps) + decay_rate * weight_float
    )
    return (stepped.astype(jnp.bfloat16), new_moment, new_second)


def tile_ranks(owner_rows):
    positions = jnp.arange(owner_rows.shape[-1], dtype=jnp.int32)
    same_owner = owner_rows[..., :, None] == owner_rows[..., None, :]
    earlier = positions[None, :] < positions[:, None]
    return jnp.sum(jnp.where(same_owner & earlier, 1, 0), axis=-1).astype(jnp.int32)


def flat_kernel(w_in, w_out, g_in, g_out, mom, sec, o_in, o_out, o_mom, o_sec):
    for m, (w, g, o) in enumerate(((w_in, g_in, o_in), (w_out, g_out, o_out))):
        new = adam_update(w[...], g[...].astype(jnp.float32), mom[m], sec[m])
        o[...], o_mom[m], o_sec[m] = new


def flat_adam(w_in, w_out, g_in, g_out, mom, sec):
    rows, width = w_in.shape
    step = min(rows, 32)
    thin = pl.BlockSpec((step, width), lambda i: (i, 0))
    wide = pl.BlockSpec((2, step, width), lambda i: (0, i, 0))
    shape = jax.ShapeDtypeStruct
    return pl.pallas_call(
        flat_kernel,
        grid=(rows // step,),
        in_specs=[thin, thin, thin, thin, wide, wide],
        out_specs=[thin, thin, wide, wide],
        out_shape=[
            shape(w_in.shape, w_in.dtype),
            shape(w_out.shape, w_out.dtype),
            shape(mom.shape, mom.dtype),
            shape(sec.shape, sec.dtype),
        ],
        cost_estimate=pl.CostEstimate(
            flops=30 * mom.size, bytes_accessed=20 * mom.size + 2 * mom.size, transcendentals=mom.size
        ),
        name="flat_adam",
    )(w_in, w_out, g_in, g_out, mom, sec)


def tile_kernel(
    tiles, live, me, l_in, l_out, r_in, r_out, w_in, w_out, mom, sec, o_in, o_out, o_mom, o_sec
):
    slot = pl.program_id(0)
    parts = ((l_in, r_in, w_in, o_in), (l_out, r_out, w_out, o_out))
    for m, (left, right, w, o) in enumerate(parts):
        grad = jnp.dot(left[...], right[0], preferred_element_type=jnp.float32)
        alive = live[m, slot] > 0
        old_w, old_m, old_s = w[0, 0], mom[m, 0, 0], sec[m, 0, 0]
        new_w, new_m, new_s = adam_update(old_w, grad, old_m, old_s)
        o[0, 0] = jnp.where(alive, new_w.astype(jnp.float32), old_w.astype(jnp.float32)).astype(
            jnp.bfloat16
        )
        o_mom[m, 0, 0] = jnp.where(alive, new_m, old_m)
        o_sec[m, 0, 0] = jnp.where(alive, new_s, old_s)


def tile_adam(tiles, live, me, l_in, l_out, r_in, r_out, w_in, w_out, mom, sec):
    slot_cap, tile_rows, width = w_in.shape[1:]
    ranks, toks, sub = r_in.shape
    step = min(sub, 512)
    per = sub // step

    def left_map(m):
        return lambda s, h, tiles, live, me: (tiles[m, s], 0)

    def right_map(s, h, tiles, live, me):
        return (lax.rem(me[0] + ranks - h // per, ranks), 0, h % per)

    def thin_map(s, h, *unused):
        return (0, s, 0, h)

    def wide_map(s, h, *unused):
        return (0, 0, s, 0, h)

    right = pl.BlockSpec((1, toks, step), right_map)
    thin = pl.BlockSpec((1, 1, tile_rows, step), thin_map)
    wide = pl.BlockSpec((2, 1, 1, tile_rows, step), wide_map)
    shape = jax.ShapeDtypeStruct
    return pl.pallas_call(
        tile_kernel,
        grid_spec=pltpu.PrefetchScalarGridSpec(
            num_scalar_prefetch=3,
            grid=(slot_cap, width // step),
            in_specs=[
                pl.BlockSpec((tile_rows, toks), left_map(0)),
                pl.BlockSpec((tile_rows, toks), left_map(1)),
                right,
                right,
                thin,
                thin,
                wide,
                wide,
            ],
            out_specs=[thin, thin, wide, wide],
        ),
        out_shape=[
            shape(w_in.shape, w_in.dtype),
            shape(w_out.shape, w_out.dtype),
            shape(mom.shape, mom.dtype),
            shape(sec.shape, sec.dtype),
        ],
        cost_estimate=pl.CostEstimate(
            flops=2 * toks * mom.size, bytes_accessed=22 * mom.size, transcendentals=mom.size
        ),
        name="tile_adam",
    )(tiles, live, me, l_in, l_out, r_in, r_out, w_in, w_out, mom, sec)


def row_swap(pieces_for, row_total):
    got = [pieces_for(0)]
    for shift in range(1, row_total):
        pairs = [(src, (src + shift) % row_total) for src in range(row_total)]
        got.append(lax.ppermute(pieces_for(shift), "row", pairs))
    return jnp.stack(got)


def spread_sum(partial, total):
    toks, width = partial.shape
    sent = partial.astype(jnp.bfloat16)
    came = lax.all_to_all(sent, both, split_axis=0, concat_axis=0, tiled=True)
    return jnp.sum(came.reshape(total, toks // total, width).astype(jnp.float32), axis=0)


def late_sum(partial):
    return lax.psum_scatter(
        partial.astype(jnp.bfloat16), both, scatter_dimension=0, tiled=True
    ).astype(jnp.float32)


def dot_nt(left, right):
    return lax.dot_general(left, right, (((1,), (1,)), ((), ())), preferred_element_type=jnp.float32)


def dot_tn(left, right):
    return lax.dot_general(left, right, (((0,), (0,)), ((), ())), preferred_element_type=jnp.float32)


def norm_of(layer_in, gain_vec):
    tok_float = layer_in.astype(jnp.float32)
    inv_rms = lax.rsqrt(jnp.mean(tok_float * tok_float, axis=1, keepdims=True) + norm_eps)
    normed = (tok_float * inv_rms * gain_vec).astype(jnp.bfloat16)
    return tok_float, inv_rms, normed


def token_grad(cotangent, d_normed, gain_vec, tok_float, inv_rms):
    gated = d_normed * gain_vec
    return (
        cotangent.astype(jnp.float32)
        + inv_rms * gated
        - tok_float
        * inv_rms
        * inv_rms
        * inv_rms
        * jnp.mean(tok_float * gated, axis=1, keepdims=True)
    ).astype(jnp.bfloat16)


def shards(
    tokens,
    grad_out,
    gains,
    flat_in,
    flat_out,
    flat_moment,
    flat_second,
    tile_in,
    tile_out,
    tile_moment,
    tile_second,
    owners,
):
    row_total = lax.axis_size("row")
    col_total = lax.axis_size("col")
    total = row_total * col_total
    row_index = lax.axis_index("row")
    model_width = tokens.shape[1]
    block = flat_in.shape[1]
    sub = block // row_total
    own_rows = flat_in.shape[0] // col_total
    slot_cap = tile_in.shape[1]
    tile_rows = tile_in.shape[2]

    owner_rows = owners[:, 0, :]
    ranks = tile_ranks(owner_rows)
    came_from = lax.rem(row_index - owner_rows + row_total, row_total)
    slot_pick = came_from * slot_cap + ranks
    slots = jnp.arange(slot_cap, dtype=jnp.int32)[None, :, None]
    mine = (owner_rows == row_index)[:, None, :] & (ranks[:, None, :] == slots)
    positions = jnp.arange(owner_rows.shape[1], dtype=jnp.int32)
    my_tiles = jnp.sum(jnp.where(mine, positions, 0), axis=-1).astype(jnp.int32)
    my_live = jnp.any(mine, axis=-1).astype(jnp.int32)

    def flat_to_units(flat):
        parts = flat.reshape(own_rows, col_total, row_total, sub).transpose(2, 1, 0, 3)
        return lax.all_to_all(
            parts.reshape(total * own_rows, sub), both, split_axis=0, concat_axis=0, tiled=True
        )

    def units_to_flat(grad):
        came = lax.all_to_all(
            grad.astype(jnp.bfloat16), both, split_axis=0, concat_axis=0, tiled=True
        )
        parts = came.reshape(row_total, col_total, own_rows, sub).transpose(2, 1, 0, 3)
        return parts.reshape(own_rows * col_total, block)

    def tiles_to_units(tile, pick):
        def piece(shift):
            to_row = lax.rem(row_index + shift, row_total)
            return lax.dynamic_slice_in_dim(tile[0], to_row * sub, sub, 2)

        whole = row_swap(piece, row_total).reshape(row_total * slot_cap, tile_rows, sub)
        return jnp.take(whole, pick, axis=0).reshape(model_width, sub)

    def gather(x):
        return lax.all_gather(x, both, axis=0, tiled=True)

    tok_one, inv_one, normed_one = norm_of(tokens, gains[0])
    normed_one = gather(normed_one)
    one_in = flat_to_units(flat_in)
    one_out = flat_to_units(flat_out)
    cot_two = gather(grad_out)
    two_in = tiles_to_units(tile_in, slot_pick[0])
    two_out = tiles_to_units(tile_out, slot_pick[1])
    hidden_one = jnp.dot(normed_one, one_in, preferred_element_type=jnp.float32)
    act_one, slope_one = gelu_both(hidden_one)
    act_one = act_one.astype(jnp.bfloat16)
    middle = (tok_one + spread_sum(dot_nt(act_one, one_out), total)).astype(jnp.bfloat16)

    tok_two, inv_two, normed_two = norm_of(middle, gains[1])
    normed_two = gather(normed_two)
    hidden_two = jnp.dot(normed_two, two_in, preferred_element_type=jnp.float32)
    act_two, slope_two = gelu_both(hidden_two)
    act_two = act_two.astype(jnp.bfloat16)
    d_act_two = jnp.dot(cot_two, two_out, preferred_element_type=jnp.float32)
    d_hidden_two = (d_act_two * slope_two).astype(jnp.bfloat16)
    d_normed_two = spread_sum(dot_nt(d_hidden_two, two_in), total)
    grad_mid = token_grad(grad_out, d_normed_two, gains[1], tok_two, inv_two)
    cot_one = gather(grad_mid)

    d_act_one = jnp.dot(cot_one, one_out, preferred_element_type=jnp.float32)
    d_hidden_one = (d_act_one * slope_one).astype(jnp.bfloat16)
    flat_grad_in = units_to_flat(dot_tn(normed_one, d_hidden_one))
    flat_grad_out = units_to_flat(dot_tn(cot_one, act_one))

    act_late, _ = lax.optimization_barrier((act_two, cot_one))
    mixed_two = late_sum(dot_nt(act_late, two_out))
    hidden_out = (tok_two + mixed_two).astype(jnp.bfloat16)
    d_normed_one = late_sum(dot_nt(d_hidden_one, one_in))
    grad_tokens = token_grad(grad_mid, d_normed_one, gains[0], tok_one, inv_one)

    d_hidden_rows = row_swap(lambda shift: d_hidden_two, row_total)
    act_rows = row_swap(lambda shift: act_two, row_total)
    new_tile = tile_adam(
        my_tiles,
        my_live,
        row_index.astype(jnp.int32).reshape(1),
        normed_two.T,
        cot_two.T,
        d_hidden_rows,
        act_rows,
        tile_in,
        tile_out,
        tile_moment,
        tile_second,
    )
    new_flat = flat_adam(flat_in, flat_out, flat_grad_in, flat_grad_out, flat_moment, flat_second)
    return (hidden_out, grad_tokens, *new_flat, *new_tile)


def solution(mesh):
    return jax.shard_map(
        shards,
        mesh=mesh,
        in_specs=(
            P(("row", "col"), None),
            P(("row", "col"), None),
            P(),
            P(("row", "col"), None),
            P(("row", "col"), None),
            P(None, ("row", "col"), None),
            P(None, ("row", "col"), None),
            P("col", "row", None, None),
            P("col", "row", None, None),
            P(None, "col", "row", None, None),
            P(None, "col", "row", None, None),
            P(None, "col", None),
        ),
        out_specs=(
            P(("row", "col"), None),
            P(("row", "col"), None),
            P(("row", "col"), None),
            P(("row", "col"), None),
            P(None, ("row", "col"), None),
            P(None, ("row", "col"), None),
            P("col", "row", None, None),
            P("col", "row", None, None),
            P(None, "col", "row", None, None),
            P(None, "col", "row", None, None),
        ),
        check_vma=False,
    )
```

time: 913 us -> 714 us (0.78); the launches traced: 901 us -> 712 us
  blocking collectives: 190 us -> 61.1 us
  other arithmetic: 115 us -> 22.4 us
  Pallas kernels: 0 us -> 55 us
  waiting for transfers between devices: 496 us -> 461 us
  local copies, waits for them, and re-layouts: 16.5 us -> 37.6 us
  matrix products: 51.5 us -> 39 us
  starting transfers between devices: 12.4 us -> 22.1 us
    reduce_scatter x6 -> x2, waiting for transfers between devices: 270 us -> 124 us  [late_sum(): lax.psum_scatter(partial.astype(jnp.bfloat16), both, scatter_dimension=0,...]
    ppermute x0 -> x4, waiting for transfers between devices: none -> 121 us  [row_swap(): got.append(lax.ppermute(pieces_for(shift), 'row', pairs))]
    all_gather x8 -> x4, waiting for transfers between devices: 222 us -> 135 us  [gather(): return lax.all_gather(x, both, axis=0, tiled=True)]
    all_gather x4 -> x0, blocking collectives: 83 us -> none  [the longest x2 43.3 us: forward(): normed_all = lax.all_gather(normed, 'col', axis=0, tiled=True)]
    all_to_all x2 -> x4, waiting for transfers between devices: 0.01 us -> 80.4 us  [the longest x2 42.8 us: flat_to_units(): lax.all_to_all(parts.reshape(total * own_rows, sub), both, split_axis=0,...]
    pallas_call x0 -> x2, Pallas kernels: none -> 55 us  [the longest x1 31.8 us: tile_adam(): pl.pallas_call(tile_kernel, grid_spec=pltpu.PrefetchScalarGridSpec(num_sc...]
    all_to_all x2, blocking collectives: 107 us -> 61.1 us  [spread_sum(): came = lax.all_to_all(sent, both, split_axis=0, concat_axis=0, tiled=True)]
    select_n x3 -> x1, other arithmetic: 42.8 us -> 3.98 us  [tiles_to_units(): return jnp.take(whole, pick, axis=0).reshape(model_width, sub)]
  transfers between devices with their start and end apart: 16 -> 14, of which waited for: 13 -> 10; matrix products, arithmetic and copies ran while one was open for 13% -> 10% of each run, Pallas kernels for 0% -> 4%
where the time goes in v1:
time: 714 us; the launch traced here: 712 us
  waiting for transfers between devices  461 us (65%)
  blocking collectives  61.1 us (9%)
  Pallas kernels  55 us (8%)
  matrix products  39 us (5%)
  local copies, waits for them, and re-layouts  37.6 us (5%)
  other arithmetic  22.4 us (3%)
  starting transfers between devices  22.1 us (3%)
  between operations  14.4 us (2%)
    all_gather x4, waiting for transfers between devices, gather(): return lax.all_gather(x, both, axis=0, tiled=True)  135 us
    reduce_scatter x2, waiting for transfers between devices, late_sum(): lax.psum_scatter(partial.astype(jnp.bfloat16), both, scatter_dimension=0,...  124 us
    ppermute x4, waiting for transfers between devices, row_swap(): got.append(lax.ppermute(pieces_for(shift), 'row', pairs))  121 us
    all_to_all x2, blocking collectives, spread_sum(): came = lax.all_to_all(sent, both, split_axis=0, concat_axis=0, tiled=True)  61.1 us
    all_to_all x2, waiting for transfers between devices, flat_to_units(): lax.all_to_all(parts.reshape(total * own_rows, sub), both, split_axis=0,...  42.8 us
    all_to_all x2, waiting for transfers between devices, units_to_flat(): lax.all_to_all(grad.astype(jnp.bfloat16), both, split_axis=0, concat_axis...  37.6 us
    pallas_call x1, Pallas kernels, tile_adam(): pl.pallas_call(tile_kernel, grid_spec=pltpu.PrefetchScalarGridSpec(num_sc...  31.8 us
    pallas_call x1, Pallas kernels, flat_adam(): pl.pallas_call(flat_kernel, grid=(rows // step,), in_specs=[thin, thin, t...  23.2 us
  transfers between devices with their start and end apart: 14, of which 10 were waited for; matrix products, arithmetic and copies ran while one was open for 10% of the time, Pallas kernels for 4%

profile of v1, /device:TPU:0, one launch (start us, length us, event | category | flops | bytes accessed | tf_op | source)
XLA Modules:
  0.0 712.4 jit_solution(11451729788757894904)
XLA Ops:
  7.2 3.3 reshape.124
  13.0 7.5 %all-to-all-start = ((bf16[32,32,1024]{2,1,0:T(8,128)(2,1)}), bf16[32,32,1024]{2,1,0:T(8,128)(2,1)}, u32[]{:S(2)}, u32[]{:S(2)}) async-start(bf16[32,32,1024]{2,1,0:T(8,128)(2,1)} %bitcast.80), calls=%async_computation | async-start | bytes 4194304 | tf_op jit(solution)/shard_map/all_to_all | solution.py:230
  23.2 4.1 copy.64
  27.2 42.8 %all-to-all-done = bf16[32,32,1024]{2,1,0:T(8,128)(2,1)} async-done(((bf16[32,32,1024]{2,1,0:T(8,128)(2,1)}), bf16[32,32,1024]{2,1,0:T(8,128)(2,1)}, u32[]{:S(2)}, u32[]{:S(2)}) %all-to-all-start) | async-done | bytes 2097184 | tf_op jit(solution)/shard_map/all_to_all | solution.py:230
  70.1 2.9 all-to-all-start.1
  73.9 64.5 %all-gather.5.cloned.1.call-done = bf16[512,1024]{1,0:T(8,128)(2,1)} async-done(((bf16[16,1024]{1,0:T(8,128)(2,1)}), bf16[512,1024]{1,0:T(8,128)(2,1)}) %all-gather.5.cloned.1.call-update) | async-done | bytes 1048592 | tf_op jit(solution)/shard_map/all_gather | solution.py:250
  138.5 4.5 fusion.32
  144.3 3.0 convolution_convert_fusion.5
  147.3 30.6 %all_to_all.60 = bf16[32,16,1024]{2,1,0:T(8,128)(2,1)S(1)} all-to-all(bf16[32,16,1024]{2,1,0:T(8,128)(2,1)S(1)} %bitcast.97), channel_id=1, replica_groups=mesh['row'=2,'col'=16] {'row','col'}, dimensions={0} | all-to-all | bytes 2097152 | tf_op jit(solution)/shard_map/all_to_all | solution.py:155
  185.6 34.0 %collective-permute-done = bf16[3,256,1024]{2,1,0:T(8,128)(2,1)S(1)} collective-permute-done((bf16[3,256,1024]{2,1,0:T(8,128)(2,1)}, bf16[3,256,1024]{2,1,0:T(8,128)(2,1)S(1)}, u32[]{:S(2)}, u32[]{:S(2)}) %collective-permute-start) | collective-permute-done | bytes 1572896 | tf_op jit(solution)/shard_map/ppermute | solution.py:148
  225.0 28.6 %collective-permute-done.1 = bf16[3,256,1024]{2,1,0:T(8,128)(2,1)} collective-permute-done((bf16[3,256,1024]{2,1,0:T(8,128)(2,1)}, bf16[3,256,1024]{2,1,0:T(8,128)(2,1)}, u32[]{:S(2)}, u32[]{:S(2)}) %collective-permute-start.1) | collective-permute-done | bytes 1572896 | tf_op jit(solution)/shard_map/ppermute | solution.py:148
  257.8 4.0 broadcast_select_fusion
  261.7 5.5 multiply_convert_fusion.1
  267.3 19.5 %all-gather.9.cloned.1.call-done = bf16[512,1024]{1,0:T(8,128)(2,1)} async-done(((bf16[16,1024]{1,0:T(8,128)(2,1)}), bf16[512,1024]{1,0:T(8,128)(2,1)}) %all-gather.9.cloned.1.call-update) | async-done | bytes 1048592 | tf_op jit(solution)/shard_map/all_gather | solution.py:250
  286.8 4.2 fusion.4
  292.3 30.6 %all_to_all.61 = bf16[32,16,1024]{2,1,0:T(8,128)(2,1)S(1)} all-to-all(bf16[32,16,1024]{2,1,0:T(8,128)(2,1)S(1)} %bitcast.96), channel_id=1, replica_groups=mesh['row'=2,'col'=16] {'row','col'}, dimensions={0} | all-to-all | bytes 2097152 | tf_op jit(solution)/shard_map/all_to_all | solution.py:155
  323.9 51.1 %all-gather.11.cloned.1.call-done = bf16[512,1024]{1,0:T(8,128)(2,1)} async-done(((bf16[16,1024]{1,0:T(8,128)(2,1)}), bf16[512,1024]{1,0:T(8,128)(2,1)}) %all-gather.11.cloned.1.call-update) | async-done | bytes 1048592 | tf_op jit(solution)/shard_map/all_gather | solution.py:250
  375.0 4.0 convolution_convert_fusion
  379.0 3.6 all-to-all-start.5
  382.6 4.6 multiply_convert_fusion
  388.2 3.9 convolution_convert_fusion.2
  392.1 4.2 convolution_convert_fusion.1
  396.3 37.6 %all-to-all-done.5 = bf16[32,32,1024]{2,1,0:T(8,128)(2,1)S(1)} async-done(((bf16[32,32,1024]{2,1,0:T(8,128)(2,1)}), bf16[32,32,1024]{2,1,0:T(8,128)(2,1)S(1)}, u32[]{:S(2)}, u32[]{:S(2)}) %all-to-all-start.5) | async-done | bytes 2097184 | tf_op jit(solution)/shard_map/all_to_all | solution.py:235
  433.9 3.5 all-to-all-start.4
  437.7 3.8 convolution_convert_fusion.3
  448.7 37.4 %collective-permute-done.2 = bf16[512,1024]{1,0:T(8,128)(2,1)} collective-permute-done((bf16[512,1024]{1,0:T(8,128)(2,1)}, bf16[512,1024]{1,0:T(8,128)(2,1)}, u32[]{:S(2)}, u32[]{:S(2)}) %collective-permute-start.2) | collective-permute-done | bytes 1048608 | tf_op jit(solution)/shard_map/ppermute | solution.py:148
  486.1 3.1 pad_maximum_fusion.2.r_in
  489.2 21.3 %collective-permute-done.3 = bf16[512,1024]{1,0:T(8,128)(2,1)} collective-permute-done((bf16[512,1024]{1,0:T(8,128)(2,1)}, bf16[512,1024]{1,0:T(8,128)(2,1)}, u32[]{:S(2)}, u32[]{:S(2)}) %collective-permute-start.3) | collective-permute-done | bytes 1048608 | tf_op jit(solution)/shard_map/ppermute | solution.py:148
  513.2 31.8 %tile_adam.1 = (bf16[1,3,256,2048]{3,2,1,0:T(8,128)(2,1)}, bf16[1,3,256,2048]{3,2,1,0:T(8,128)(2,1)}, f32[2,1,3,256,2048]{4,3,2,1,0:T(8,128)}, f32[2,1,3,256,2048]{4,3,2,1,0:T(8,128)}) custom-call(s32[2,3]{1,0:T(2,128)} %select_reduce_fusion.tiles, s32[2,3]{1,0:T(2,128)} %convert_element_type.99.live, s32[1]{0:T(128)} %bitcast.28.me, ...), custom_call_target="tpu_custom_call" | custom-call | flops 3221225472 | bytes 69206016 | tf_op jit(solution)/shard_map/tile_adam/pallas_call | solution.py:114
  546.0 123.8 %reduce-scatter.7.cloned.1.call-done = bf16[16,1024]{1,0:T(8,128)(2,1)} async-done(((bf16[512,1024]{1,0:T(8,128)(2,1)}), bf16[16,1024]{1,0:T(8,128)(2,1)}) %reduce-scatter.7.cloned.1.call-update) | async-done | bytes 32784 | tf_op jit(solution)/shard_map/reduce_scatter | solution.py:160
  676.7 3.7 copy.70
  682.4 23.2 %flat_adam.1 = (bf16[512,2048]{1,0:T(8,128)(2,1)}, bf16[512,2048]{1,0:T(8,128)(2,1)}, f32[2,512,2048]{2,1,0:T(8,128)}, f32[2,512,2048]{2,1,0:T(8,128)}) custom-call(bf16[512,2048]{1,0:T(8,128)(2,1)} %w_in.2, bf16[512,2048]{1,0:T(8,128)(2,1)} %w_out.2, bf16[512,2048]{1,0:T(8,128)(2,1)} %bitcast.78, bf16[512,2048]{1,0:T(8,128)(2,1)} %bitcast.77, ...), custom_call_target="tpu_custom_call" | custom-call | flops 62914560 | bytes 46137344 | tf_op jit(solution)/shard_map/flat_adam/pallas_call | solution.py:57
  (98 shorter events, 47.9 us)
Async XLA Ops:
  13.0 7.5 %copy-start.2 = (bf16[512,2048]{1,0:T(8,128)(2,1)S(1)}, bf16[512,2048]{1,0:T(8,128)(2,1)}, u32[]{:S(2)}) copy-start(bf16[512,2048]{1,0:T(8,128)(2,1)} %w_out.2) | copy-start | bytes 6291460
  13.0 57.1 %all-to-all-start = ((bf16[32,32,1024]{2,1,0:T(8,128)(2,1)}), bf16[32,32,1024]{2,1,0:T(8,128)(2,1)}, u32[]{:S(2)}, u32[]{:S(2)}) async-start(bf16[32,32,1024]{2,1,0:T(8,128)(2,1)} %bitcast.80), calls=%async_computation | async-start | bytes 4194304 | tf_op jit(solution)/shard_map/all_to_all | solution.py:230
  70.1 2.9 copy-start.11
  70.1 3.1 copy-start.15
  70.1 72.9 %all-to-all-start.1 = ((bf16[32,32,1024]{2,1,0:T(8,128)(2,1)}), bf16[32,32,1024]{2,1,0:T(8,128)(2,1)S(1)}, u32[]{:S(2)}, u32[]{:S(2)}) async-start(bf16[32,32,1024]{2,1,0:T(8,128)(2,1)} %bitcast.5), calls=%async_computation.1 | async-start | bytes 4194304 | tf_op jit(solution)/shard_map/all_to_all | solution.py:230
  73.0 65.5 %all-gather.5.cloned.1.call-start = ((), (), s32[]{:S(2)}) async-start(), calls=%async_computation.8 | async-start | bytes 1081344 | tf_op jit(solution)/shard_map/all_gather | solution.py:250
  73.9 187.9 %all-gather.7.cloned.1.call-start = ((), (), s32[]{:S(2)}) async-start(), calls=%async_computation.9 | async-start | bytes 1081344 | tf_op jit(solution)/shard_map/all_gather | solution.py:250
  143.0 1.3 copy-start.5
  147.3 31.7 %copy-start.1 = (bf16[1,3,256,2048]{3,2,1,0:T(8,128)(2,1)S(1)}, bf16[1,3,256,2048]{3,2,1,0:T(8,128)(2,1)}, u32[]{:S(2)}) copy-start(bf16[1,3,256,2048]{3,2,1,0:T(8,128)(2,1)} %w_in.3) | copy-start | bytes 9437188
  178.9 107.9 %all-gather.9.cloned.1.call-start = ((), (), s32[]{:S(2)}) async-start(), calls=%async_computation.10 | async-start | bytes 1081344 | tf_op jit(solution)/shard_map/all_gather | solution.py:250
  179.0 3.0 copy-start
  181.1 4.3 copy-start.14
  181.1 38.6 %collective-permute-start = (bf16[3,256,1024]{2,1,0:T(8,128)(2,1)}, bf16[3,256,1024]{2,1,0:T(8,128)(2,1)S(1)}, u32[]{:S(2)}, u32[]{:S(2)}) collective-permute-start(bf16[3,256,1024]{2,1,0:T(8,128)(2,1)} %get-tuple-element.68), channel_id=1, source_target_pairs={{0,16},{16,0},{1,17},{17,1},{2,18},{18,2},{3,19},{19,3},{4,20},{20... | collective-permute-start | bytes 4718600 | tf_op jit(solution)/shard_map/ppermute | solution.py:148
  184.0 69.6 %collective-permute-start.1 = (bf16[3,256,1024]{2,1,0:T(8,128)(2,1)}, bf16[3,256,1024]{2,1,0:T(8,128)(2,1)}, u32[]{:S(2)}, u32[]{:S(2)}) collective-permute-start(bf16[3,256,1024]{2,1,0:T(8,128)(2,1)} %get-tuple-element.66), channel_id=1, source_target_pairs={{0,16},{16,0},{1,17},{17,1},{2,18},{18,2},{3,19},{19,3},{4,20},{20... | collective-permute-start | bytes 4718600 | tf_op jit(solution)/shard_map/ppermute | solution.py:148
  185.1 189.9 %all-gather.11.cloned.1.call-start = ((), (), s32[]{:S(2)}) async-start(), calls=%async_computation.11 | async-start | bytes 1081344 | tf_op jit(solution)/shard_map/all_gather | solution.py:250
  219.7 1.1 copy-start.6
  261.7 25.1 %copy-start.3 = (bf16[4,256,1024]{2,1,0:T(8,128)(2,1)}, bf16[4,256,1024]{2,1,0:T(8,128)(2,1)S(1)}, u32[]{:S(2)}) copy-start(bf16[4,256,1024]{2,1,0:T(8,128)(2,1)S(1)} %get-tuple-element.75) | copy-start | bytes 6291460
  267.3 170.4 %copy-start.8 = (bf16[512,1024]{1,0:T(8,128)(2,1)}, bf16[512,1024]{1,0:T(8,128)(2,1)S(1)}, u32[]{:S(2)}) copy-start(bf16[512,1024]{1,0:T(8,128)(2,1)S(1)} %get-tuple-element.20) | copy-start | bytes 3145732
  286.8 4.2 copy-start.4
  291.0 1.3 copy-start.10
  292.3 30.9 %copy-start.13 = (bf16[16,1024]{1,0:T(8,128)(2,1)S(1)}, bf16[16,1024]{1,0:T(8,128)(2,1)}, u32[]{:S(2)}) copy-start(bf16[16,1024]{1,0:T(8,128)(2,1)} %param.15) | copy-start | bytes 98308
  292.3 82.7 %copy-start.16 = (f32[512,1024]{1,0:T(8,128)S(1)}, f32[512,1024]{1,0:T(8,128)}, u32[]{:S(2)}) copy-start(f32[512,1024]{1,0:T(8,128)} %fusion.32) | copy-start | bytes 6291460
  379.0 54.9 %all-to-all-start.5 = ((bf16[32,32,1024]{2,1,0:T(8,128)(2,1)}), bf16[32,32,1024]{2,1,0:T(8,128)(2,1)S(1)}, u32[]{:S(2)}, u32[]{:S(2)}) async-start(bf16[32,32,1024]{2,1,0:T(8,128)(2,1)} %bitcast.94), calls=%async_computation.5 | async-start | bytes 4194304 | tf_op jit(solution)/shard_map/all_to_all | solution.py:235
  382.6 162.5 %reduce-scatter.9.cloned.1.call-start = ((), (), s32[]{:S(2)}) async-start(), calls=%async_computation.13 | async-start | bytes 1081344 | tf_op jit(solution)/shard_map/reduce_scatter | solution.py:160
  387.3 1.0 copy-start.17
  433.9 242.8 %all-to-all-start.4 = ((bf16[32,32,1024]{2,1,0:T(8,128)(2,1)}), bf16[32,32,1024]{2,1,0:T(8,128)(2,1)}, u32[]{:S(2)}, u32[]{:S(2)}) async-start(bf16[32,32,1024]{2,1,0:T(8,128)(2,1)} %bitcast.93), calls=%async_computation.4 | async-start | bytes 4194304 | tf_op jit(solution)/shard_map/all_to_all | solution.py:235
  437.4 232.4 %reduce-scatter.7.cloned.1.call-start = ((), (), s32[]{:S(2)}) async-start(), calls=%async_computation.12 | async-start | bytes 1081344 | tf_op jit(solution)/shard_map/reduce_scatter | solution.py:160
  441.5 5.8 copy-start.7
  441.5 44.6 %collective-permute-start.2 = (bf16[512,1024]{1,0:T(8,128)(2,1)}, bf16[512,1024]{1,0:T(8,128)(2,1)}, u32[]{:S(2)}, u32[]{:S(2)}) collective-permute-start(bf16[512,1024]{1,0:T(8,128)(2,1)} %copy-done.10), channel_id=1, source_target_pairs={{0,16},{16,0},{1,17},{17,1},{2,18},{18,2},{3,19},{19,3},{4,20},{20... | collective-permute-start | bytes 3145736 | tf_op jit(solution)/shard_map/ppermute | solution.py:148
  443.2 67.3 %collective-permute-start.3 = (bf16[512,1024]{1,0:T(8,128)(2,1)}, bf16[512,1024]{1,0:T(8,128)(2,1)}, u32[]{:S(2)}, u32[]{:S(2)}) collective-permute-start(bf16[512,1024]{1,0:T(8,128)(2,1)} %copy-done.8), channel_id=1, source_target_pairs={{0,16},{16,0},{1,17},{17,1},{2,18},{18,2},{3,19},{19,3},{4,20},{20... | collective-permute-start | bytes 3145736 | tf_op jit(solution)/shard_map/ppermute | solution.py:148
  486.1 24.4 %copy-start.9 = (bf16[512,1024]{1,0:T(8,128)(2,1)S(1)}, bf16[512,1024]{1,0:T(8,128)(2,1)}, u32[]{:S(2)}) copy-start(bf16[512,1024]{1,0:T(8,128)(2,1)} %copy-done.8) | copy-start | bytes 3145732
  513.2 157.9 %copy-start.12 = (bf16[16,1024]{1,0:T(8,128)(2,1)S(1)}, bf16[16,1024]{1,0:T(8,128)(2,1)}, u32[]{:S(2)}) copy-start(bf16[16,1024]{1,0:T(8,128)(2,1)} %fusion.13) | copy-start | bytes 98308
Sparse Core Ops, SparseCore 0:
  77.2 61.2 all-gather.4
  179.0 52.1 all-gather.6
  234.1 52.6 all-gather.8
  324.0 50.9 all-gather.10
  392.2 141.6 reduce-scatter.8
  536.6 133.1 reduce-scatter.6
